TPU v7x, 128 devices: a whole 4x4x4 slice. The times are simulated.
128 devices in a mesh: slab: 8 (over x, y_lo), tile: 16 (over y_hi, z, core).
Axes of the slice: x: 4, y: 4 (y_hi: 2, y_lo: 2; y = y_hi * 2 + y_lo), z: 4, core: 2. Of those that a mesh axis runs over, the one named last changes fastest.
Arguments:
- distribution_functions: float32 [19, 128, 512, 128], P(None, 'slab', 'tile')
- heat_excess_scalar: float32 [128, 512, 128], P('slab', 'tile'), may hold values from -6 to 6
- obstacle_site_flag: int32 [128, 512, 128], P('slab', 'tile'), may hold values from 0 to 1, as said below
- cabinet_category_label: int32 [1024], replicated, may hold values from 0 to 7
- intake_face_position: int32 [1024, 32], replicated, may hold values from 0 to 8388607, as said below
- outflow_face_position: int32 [1024, 32], replicated, may hold values from 0 to 8388607, as said below
- category_evolution_operator: bfloat16 [8, 2048, 2048], P(None, 'tile', 'slab'), may hold values from -0.125 to 0.125
- intake_input_coefficients: float32 [8, 2048], replicated, may hold values from -12 to 12
- outflow_output_coefficients: float32 [8, 2048], replicated, may hold values from -0.125 to 0.125
- cabinet_heat_vector: bfloat16 [1024, 2048], P('slab'), may hold values from -6 to 6
Outputs:
- new_populations: float32 [19, 128, 512, 128], P(None, 'slab', 'tile')
- new_temperature: float32 [128, 512, 128], P('slab', 'tile')
- new_states: float32 [1024, 2048], P('slab', 'tile')
Inputs may be any that keep to these rules, and one draw needn't show every extreme that they name: `intake_face_position`: each rack is a block 4 cells wide and 8 high in a row of racks along the hall; its inlet face, body and exhaust face lie in three consecutive cells along the hall's length, all within one slab of 16 cells. No cell belongs to two faces; face cells are never solid. `outflow_face_position`: same layout as the inlet faces, two cells further along the hall. `obstacle_site_flag`: the lowest and highest layer of cells and every rack body are solid.
All inputs are finite; a program needn't handle non-finite values.
Results may differ from a plain program's by a relative error of at most 0.00085.
Values may be sent and summed in bfloat16 or wider, within the bound.
A program may use at most 128 MiB of HBM per device.

v0:
```python
import jax
import jax.numpy as jnp
from jax import lax
from jax.sharding import PartitionSpec as P

STEPS = 3
VELOCITY = (
    (0, 0, 0),
    (1, 0, 0),
    (-1, 0, 0),
    (0, 1, 0),
    (0, -1, 0),
    (0, 0, 1),
    (0, 0, -1),
    (1, 1, 0),
    (-1, -1, 0),
    (1, -1, 0),
    (-1, 1, 0),
    (1, 0, 1),
    (-1, 0, -1),
    (1, 0, -1),
    (-1, 0, 1),
    (0, 1, 1),
    (0, -1, -1),
    (0, 1, -1),
    (0, -1, 1),
)
OPPOSITE = (0, 2, 1, 4, 3, 6, 5, 8, 7, 10, 9, 12, 11, 14, 13, 16, 15, 18, 17)
WEIGHTS = (1.0 / 3.0,) + (1.0 / 18.0,) * 6 + (1.0 / 36.0,) * 12
relax_time = 0.6
buoyancy = 0.01
diffusion = 0.1
mixing = 0.5
keep_share = 0.5


def extended(cells, sides, width):
    for axis, dim in sides:
        count = lax.axis_size(axis)
        head = lax.slice_in_dim(cells, 0, width, axis=dim)
        tail = lax.slice_in_dim(cells, cells.shape[dim] - width, cells.shape[dim], axis=dim)
        cells = jnp.concatenate(
            [
                lax.ppermute(tail, axis, [(i, (i + 1) % count) for i in range(count)]),
                cells,
                lax.ppermute(head, axis, [((i + 1) % count, i) for i in range(count)]),
            ],
            axis=dim,
        )
    return cells


def collide(lattice_quantities, heated_quantities, solid):
    density = jnp.sum(lattice_quantities, axis=0)
    velocity = []
    for dimension in range(3):
        summed = jnp.zeros_like(density)
        for lane in range(19):
            stride = VELOCITY[lane][dimension]
            if stride != 0:
                summed = summed + stride * lattice_quantities[lane]
        velocity.append(summed / density)
    shifted = [
        velocity[0],
        velocity[1],
        velocity[2] + relax_time * buoyancy * heated_quantities / density,
    ]
    speed_sq = shifted[0] * shifted[0] + shifted[1] * shifted[1] + shifted[2] * shifted[2]
    relaxed = []
    for lane in range(19):
        stride = VELOCITY[lane]
        projected = stride[0] * shifted[0] + stride[1] * shifted[1] + stride[2] * shifted[2]
        balance = (
            WEIGHTS[lane]
            * density
            * (1.0 + 3.0 * projected + 4.5 * projected * projected - 1.5 * speed_sq)
        )
        relaxed_lane = lattice_quantities[lane] - (lattice_quantities[lane] - balance) / relax_time
        relaxed.append(jnp.where(solid, lattice_quantities[OPPOSITE[lane]], relaxed_lane))
    return (jnp.stack(relaxed), velocity)


def heat_step(centre, neighbours, velocity, solid):
    laplace = -6.0 * centre
    carried = jnp.zeros_like(centre)
    for dimension in range(3):
        behind, ahead = neighbours[dimension]
        laplace = laplace + behind + ahead
        carried = carried + velocity[dimension] * (0.5 * (ahead - behind))
    return jnp.where(solid, centre, centre + diffusion * laplace - carried)


def advance(relaxed_pad, heat_pad, velocity, solid):
    size_x = solid.shape[0]
    size_y = solid.shape[1]
    passed = []
    for lane in range(19):
        stride = VELOCITY[lane]
        moved = relaxed_pad[
            lane, 1 - stride[0] : 1 - stride[0] + size_x, 1 - stride[1] : 1 - stride[1] + size_y
        ]
        passed.append(jnp.roll(moved, stride[2], axis=2))
    centre = heat_pad[1 : 1 + size_x, 1 : 1 + size_y]
    neighbours = (
        (heat_pad[0:size_x, 1 : 1 + size_y], heat_pad[2 : 2 + size_x, 1 : 1 + size_y]),
        (heat_pad[1 : 1 + size_x, 0:size_y], heat_pad[1 : 1 + size_x, 2 : 2 + size_y]),
        (jnp.roll(centre, 1, axis=2), jnp.roll(centre, -1, axis=2)),
    )
    return (jnp.stack(passed), heat_step(centre, neighbours, velocity, solid))


def select(products, kind_hot, rows_here):
    shaped = products.reshape(products.shape[0], kind_hot.shape[1], rows_here)
    return jnp.sum(shaped * kind_hot[:, :, None], axis=1)


def per_device(
    distribution_functions,
    heat_excess_scalar,
    obstacle_site_flag,
    cabinet_category_label,
    intake_face_position,
    outflow_face_position,
    category_evolution_operator,
    intake_input_coefficients,
    outflow_output_coefficients,
    cabinet_heat_vector,
):
    solid = obstacle_site_flag == 1
    lattice_quantities, heated_quantities = (distribution_functions, heat_excess_scalar)
    for substep in range(STEPS):
        relaxed, velocity = collide(lattice_quantities, heated_quantities, solid)
        stacked = jnp.concatenate((relaxed, heated_quantities[None]), axis=0)
        padded = extended(stacked, (("slab", 1), ("tile", 2)), 1)
        lattice_quantities, heated_quantities = advance(padded[:19], padded[19], velocity, solid)
    slab_index = lax.axis_index("slab")
    tile_index = lax.axis_index("tile")
    size_x, size_y, height = heated_quantities.shape
    across_total = size_y * lax.axis_size("tile")
    block_racks = cabinet_heat_vector.shape[0]
    kinds_count = category_evolution_operator.shape[0]
    rows_here = category_evolution_operator.shape[1]
    first_rack = slab_index * block_racks
    kind_range = jnp.arange(kinds_count, dtype=jnp.int32)
    block_types = lax.dynamic_slice_in_dim(cabinet_category_label, first_rack, block_racks)
    kind_hot = (block_types[:, None] == kind_range[None, :]).astype(jnp.float32)

    def locate(face_cells):
        pos_x = face_cells // (across_total * height)
        remain = face_cells % (across_total * height)
        pos_y = remain // height
        pos_z = remain % height
        owned = (pos_x // size_x == slab_index) & (pos_y // size_y == tile_index)
        local_index = (
            (pos_x - slab_index * size_x) * size_y + (pos_y - tile_index * size_y)
        ) * height + pos_z
        return (owned, jnp.where(owned, local_index, 0))

    flat_heat = heated_quantities.reshape(-1)
    block_inlet = lax.dynamic_slice_in_dim(intake_face_position, first_rack, block_racks, 0)
    inlet_owned, inlet_index = locate(block_inlet)
    partial_inlet = jnp.sum(jnp.where(inlet_owned, flat_heat[inlet_index], 0.0), axis=1)
    inlet_mean = lax.psum(partial_inlet, "tile") / intake_face_position.shape[1]
    piece_cols = lax.all_gather(category_evolution_operator, "slab", axis=2, tiled=True)
    flat_piece = piece_cols.reshape(kinds_count * rows_here, piece_cols.shape[2])
    all_kinds = lax.dot_general(
        cabinet_heat_vector,
        flat_piece,
        (((1,), (1,)), ((), ())),
        preferred_element_type=jnp.float32,
    )
    mixed = select(all_kinds, kind_hot, rows_here)
    first_row = tile_index * rows_here
    state_rows = lax.dynamic_slice_in_dim(cabinet_heat_vector, first_row, rows_here, 1).astype(
        jnp.float32
    )
    gain_table = lax.dynamic_slice_in_dim(intake_input_coefficients, first_row, rows_here, 1)
    read_table = lax.dynamic_slice_in_dim(outflow_output_coefficients, first_row, rows_here, 1)
    gain_rows = jnp.dot(kind_hot, gain_table, precision=lax.Precision.HIGHEST)
    read_rows = jnp.dot(kind_hot, read_table, precision=lax.Precision.HIGHEST)
    new_states = keep_share * state_rows + mixed + gain_rows * inlet_mean[:, None]
    partial_exhaust = jnp.sum(read_rows * new_states, axis=1)
    exhaust = lax.psum(partial_exhaust, "tile")
    block_exhaust = lax.dynamic_slice_in_dim(outflow_face_position, first_rack, block_racks, 0)
    exhaust_owned, exhaust_index = locate(block_exhaust)
    old_values = flat_heat[exhaust_index]
    change = jnp.where(exhaust_owned, mixing * (exhaust[:, None] - old_values), 0.0)
    flat_heat = flat_heat.at[exhaust_index.reshape(-1)].add(change.reshape(-1))
    return (lattice_quantities, flat_heat.reshape(heated_quantities.shape), new_states)


def solution(mesh):
    return jax.shard_map(
        per_device,
        mesh=mesh,
        in_specs=(
            P(None, "slab", "tile", None),
            P("slab", "tile", None),
            P("slab", "tile", None),
            P(),
            P(),
            P(),
            P(None, "tile", "slab"),
            P(),
            P(),
            P("slab", None),
        ),
        out_specs=(P(None, "slab", "tile", None), P("slab", "tile", None), P("slab", "tile")),
        check_vma=False,
    )
```

profile of v0, /device:TPU:7, one launch (start us, length us, event | category | flops | bytes accessed | tf_op | source)
XLA Modules:
  0.0 359.1 jit_solution(3612530613693756231)
XLA Ops:
  7.2 3.0 reduce_sum.184
  10.3 4.1 %bitcast_dynamic-update-slice_fusion.10 = (f32[20,16,32,128]{3,2,1,0:T(8,128)S(1)}, f32[16,32,128]{2,1,0:T(8,128)}, f32[16,32,128]{2,1,0:T(8,128)S(1)}, f32[16,3...) fusion(f32[16,32,128]{2,1,0:T(8,128)S(1)} %reduce_sum.184, ...), kind=kLoop, calls=%fused_computation.703 | loop fusion | flops 4521983 | bytes 7667712
  14.4 1.2 fusion.20
  19.7 2.3 copy-done.4
  22.1 1.4 collective-permute-start
  23.5 1.1 collective-permute-start.1
  25.4 0.9 compare_select_fusion
  26.9 15.5 %collective-permute-done = f32[20,1,32,128]{3,2,1,0:T(8,128)S(1)} collective-permute-done((f32[20,1,32,128]{3,2,1,0:T(8,128)S(1)}, f32[20,1,32,128]{3,2,1,0:T(8,128)S(1)}, u32[]{:S(2)}, u32[]{:S(2)}) %collective-permute-start) | collective-permute-done | bytes 327712 | tf_op jit(solution)/shard_map/ppermute | solution.py:44
  42.5 4.2 %collective-permute-done.1 = f32[20,1,32,128]{3,2,1,0:T(8,128)S(1)} collective-permute-done((f32[20,1,32,128]{3,2,1,0:T(8,128)S(1)}, f32[20,1,32,128]{3,2,1,0:T(8,128)S(1)}, u32[]{:S(2)}, u32[]{:S(2)}) %collective-permute-start.1) | collective-permute-done | bytes 327712 | tf_op jit(solution)/shard_map/ppermute | solution.py:46
  46.7 2.9 pad_maximum_fusion.70
  49.5 2.5 collective-permute-start.2
  52.7 0.8 slice.921
  53.6 0.8 slice.919
  55.1 1.4 fusion.507
  57.7 0.7 fusion.6
  58.8 1.0 fusion.505
  60.5 4.0 %bitcast_dynamic-update-slice_fusion.6 = (f32[20,16,32,128]{3,2,1,0:T(8,128)S(1)}, f32[16,32,128]{2,1,0:T(8,128)}, f32[16,32,128]{2,1,0:T(8,128)S(1)}, f32[16,32...) fusion(pred[16,32,128]{2,1,0:T(8,128)(4,1)S(1)} %get-tuple-elem, ...), kind=kLoop, calls=%fused_computation.699 | loop fusion | flops 9175039 | bytes 18653184
  68.7 2.3 copy-done.3
  71.0 1.7 collective-permute-start.4
  72.7 0.8 collective-permute-start.5
  73.5 0.8 compare_select_fusion.1
  75.1 12.0 %collective-permute-done.4 = f32[20,1,32,128]{3,2,1,0:T(8,128)S(1)} collective-permute-done((f32[20,1,32,128]{3,2,1,0:T(8,128)S(1)}, f32[20,1,32,128]{3,2,1,0:T(8,128)S(1)}, u32[]{:S(2)}, u32[]{:S(2)}) %collective-permute-start.4) | collective-permute-done | bytes 327712 | tf_op jit(solution)/shard_map/ppermute | solution.py:44
  87.1 9.8 %collective-permute-done.5 = f32[20,1,32,128]{3,2,1,0:T(8,128)S(1)} collective-permute-done((f32[20,1,32,128]{3,2,1,0:T(8,128)S(1)}, f32[20,1,32,128]{3,2,1,0:T(8,128)S(1)}, u32[]{:S(2)}, u32[]{:S(2)}) %collective-permute-start.5) | collective-permute-done | bytes 327712 | tf_op jit(solution)/shard_map/ppermute | solution.py:46
  96.9 2.8 pad_maximum_fusion.67
  99.7 12.5 %collective-permute-start.6 = (f32[20,18,1,128]{3,2,1,0:T(1,128)}, f32[20,18,1,128]{3,2,1,0:T(1,128)S(1)}, u32[]{:S(2)}, u32[]{:S(2)}) collective-permute-start(f32[20,18,1,128]{3,2,1,0:T(1,128)} %get-tuple-element.107), channel_id=1, source_target_pairs={{0,1},{1,2},{2,3},{3,4},{4,5},{5,6},{6,7},{7,8},{8,9},{9,10},{10,1... | collective-permute-start | bytes 552968 | tf_op jit(solution)/shard_map/ppermute | solution.py:44
  112.8 0.8 dynamic_slice.19
  113.6 1.5 copy.25
  115.3 1.4 fusion.503
  117.9 0.7 fusion.5
  119.0 1.0 fusion.501
  120.7 3.4 constant_dynamic-update-slice_fusion
  128.3 6.5 %collective-permute-start.9 = (f32[20,1,32,128]{3,2,1,0:T(8,128)S(1)}, f32[20,1,32,128]{3,2,1,0:T(8,128)S(1)}, u32[]{:S(2)}, u32[]{:S(2)}) collective-permute-start(f32[20,1,32,128]{3,2,1,0:T(8,128)S(1)} %get-tuple-element.123), channel_id=1, source_target_pairs={{16,0},{32,16},{48,32},{64,48},{80,64},{96,80},{112,96},{0,112},{1... | collective-permute-start | bytes 983048 | tf_op jit(solution)/shard_map/ppermute | solution.py:46
  134.8 0.8 slice.981
  136.5 9.8 %collective-permute-done.8 = f32[20,1,32,128]{3,2,1,0:T(8,128)S(1)} collective-permute-done((f32[20,1,32,128]{3,2,1,0:T(8,128)S(1)}, f32[20,1,32,128]{3,2,1,0:T(8,128)S(1)}, u32[]{:S(2)}, u32[]{:S(2)}) %collective-permute-start.8) | collective-permute-done | bytes 327712 | tf_op jit(solution)/shard_map/ppermute | solution.py:44
  146.2 2.6 collective-permute-done.9
  149.1 2.3 collective-permute-start.10
  151.4 13.0 %collective-permute-start.11 = (f32[20,18,1,128]{3,2,1,0:T(1,128)S(1)}, f32[20,18,1,128]{3,2,1,0:T(1,128)S(1)}, u32[]{:S(2)}, u32[]{:S(2)}) collective-permute-start(f32[20,18,1,128]{3,2,1,0:T(1,128)S(1)} %get-tuple-element.103), channel_id=1, source_target_pairs={{1,0},{2,1},{3,2},{4,3},{5,4},{6,5},{7,6},{8,7},{9,8},{10,9},{11,1... | collective-permute-start | bytes 552968 | tf_op jit(solution)/shard_map/ppermute | solution.py:46
  166.6 23.0 %gather_fusion = f32[4096]{0:T(1024)S(1)} fusion(f32[65536]{0:T(1024)S(1)} %bitcast.598, s32[4096]{0:T(1024)S(1)} %copy-done.24), kind=kCustom, calls=%fused_computation | custom fusion | bytes 49152 | tf_op jit(solution)/shard_map/gather | solution.py:162
  189.7 23.0 %gather_fusion.1 = f32[4096]{0:T(1024)S(1)} fusion(f32[65536]{0:T(1024)S(1)} %bitcast.599, s32[4096]{0:T(1024)S(1)} %get-tuple-element.143), kind=kCustom, calls=%fused_computation.1 | custom fusion | bytes 49152 | tf_op jit(solution)/shard_map/gather | solution.py:186
  212.9 1.8 maximum_dynamic-update-slice_fusion.5
  214.7 1.8 maximum_dynamic-update-slice_fusion.4
  216.5 0.8 fusion.509
  217.3 0.8 fusion.510
  219.6 0.9 fusion.497
  220.5 0.8 slice.985
  221.3 0.8 fusion.498
  222.2 0.8 slice.987
  223.0 0.8 slice.989
  223.9 0.8 slice.991
  224.7 0.8 slice.993
  226.1 39.8 %psum.14 = f32[128]{0:T(128)S(1)} all-reduce(f32[128]{0:T(128)S(1)} %select_reduce_fusion), channel_id=1, replica_groups=mesh['slab'=8,'tile'=16] {'tile'}, use_global_device_ids=true, to_apply=%region_3.4 | all-reduce | flops 128 | bytes 1024 | tf_op jit(solution)/shard_map/psum | solution.py:163
  265.9 1.9 fusion.511
  267.8 1.9 fusion.512
  269.7 1.8 fusion.513
  271.5 1.8 fusion.514
  273.2 1.8 fusion.515
  275.0 0.8 fusion.516
  275.9 0.8 fusion.517
  276.7 0.8 fusion.518
  277.6 3.7 %fusion = f32[128,128]{1,0:T(8,128)S(1)} fusion(bf16[8,128,2048]{2,1,0:T(8,128)(2,1)} %all-gather.2.cloned.1.call-done, bf16[128,2048]{1,0:T(8,128)(2,1)S(1)} %copy-done, f32[128,8]{0,1:T(8,128)S(1)} %fusion.571), kind=kOutput, calls=%fused_computation.4 | convolution fusion | flops 537116672 | bytes 4788224 | tf_op jit(solution)/shard_map/dot_general | solution.py:166
  281.4 0.9 fusion.1
  283.1 1.0 fusion.2
  284.0 38.5 %psum.15 = f32[128]{0:T(128)S(1)} all-reduce(f32[128]{0:T(128)S(1)} %fusion.2), channel_id=1, replica_groups=mesh['slab'=8,'tile'=16] {'tile'}, use_global_device_ids=true, to_apply=%region_5.6 | all-reduce | flops 128 | bytes 1024 | tf_op jit(solution)/shard_map/psum | solution.py:183
  322.7 28.9 %scatter_fusion = f32[65536]{0:T(1024)S(1)} fusion(f32[65536]{0:T(1024)S(1)} %bitcast.600, s32[4096]{0:T(1024)S(1)} %bitcast.638, f32[4096]{0:T(1024)S(1)} %reshape.165), kind=kCustom, calls=%fused_computation.2 | custom fusion | flops 4096 | bytes 65536 | tf_op jit(solution)/shard_map/scatter-add | solution.py:188
  (203 shorter events, 28.1 us)
Async XLA Ops:
  7.2 105.0 %copy-start = (bf16[128,2048]{1,0:T(8,128)(2,1)S(1)}, bf16[128,2048]{1,0:T(8,128)(2,1)}, u32[]{:S(2)}) copy-start(bf16[128,2048]{1,0:T(8,128)(2,1)} %param.19) | copy-start | bytes 1572868
  7.2 3.1 copy-start.23
  7.2 3.1 copy-start.27
  7.2 270.4 %all-gather.2.cloned.1.call-start = ((), (), s32[]{:S(2)}) async-start(), calls=%async_computation | async-start | bytes 4718592 | tf_op jit(solution)/shard_map/all_gather | solution.py:164
  10.3 5.3 %copy-start.5 = (f32[19,16,32,128]{3,2,1,0:T(8,128)S(1)}, f32[19,16,32,128]{3,2,1,0:T(8,128)}, u32[]{:S(2)}) copy-start(f32[19,16,32,128]{3,2,1,0:T(8,128)} %param.10) | copy-start | bytes 14942212
  16.6 37.0 %copy-start.6 = (f32[16,32,128]{2,1,0:T(8,128)}, f32[16,32,128]{2,1,0:T(8,128)S(1)}, u32[]{:S(2)}) copy-start(f32[16,32,128]{2,1,0:T(8,128)S(1)} %get-tuple-element.80) | copy-start | bytes 786436
  16.8 35.9 %copy-start.10 = (f32[16,32,128]{2,1,0:T(8,128)}, f32[16,32,128]{2,1,0:T(8,128)S(1)}, u32[]{:S(2)}) copy-start(f32[16,32,128]{2,1,0:T(8,128)S(1)} %get-tuple-element.78) | copy-start | bytes 786436
  19.7 2.3 copy-start.4
  22.1 20.4 %collective-permute-start = (f32[20,1,32,128]{3,2,1,0:T(8,128)S(1)}, f32[20,1,32,128]{3,2,1,0:T(8,128)S(1)}, u32[]{:S(2)}, u32[]{:S(2)}) collective-permute-start(f32[20,1,32,128]{3,2,1,0:T(8,128)S(1)} %get-tuple-element.129), channel_id=1, source_target_pairs={{0,16},{16,32},{32,48},{48,64},{64,80},{80,96},{96,112},{112,0},{1... | collective-permute-start | bytes 983048 | tf_op jit(solution)/shard_map/ppermute | solution.py:44
  23.5 23.2 %collective-permute-start.1 = (f32[20,1,32,128]{3,2,1,0:T(8,128)S(1)}, f32[20,1,32,128]{3,2,1,0:T(8,128)S(1)}, u32[]{:S(2)}, u32[]{:S(2)}) collective-permute-start(f32[20,1,32,128]{3,2,1,0:T(8,128)S(1)} %get-tuple-element.130), channel_id=1, source_target_pairs={{16,0},{32,16},{48,32},{64,48},{80,64},{96,80},{112,96},{0,112},{1... | collective-permute-start | bytes 983048 | tf_op jit(solution)/shard_map/ppermute | solution.py:46
  46.7 10.9 %slice-start.4 = ((s8[5242880]{0:T(1024)(128)(4,1)}), s8[1048576]{0:T(1024)(128)(4,1)S(1)}, s32[]{:S(2)}) async-start(s8[5242880]{0:T(1024)(128)(4,1)} %bitcast.606), calls=%async_computation.5 | async-start | bytes 2097152
  49.5 7.4 %collective-permute-start.2 = (f32[20,18,1,128]{3,2,1,0:T(1,128)}, f32[20,18,1,128]{3,2,1,0:T(1,128)S(1)}, u32[]{:S(2)}, u32[]{:S(2)}) collective-permute-start(f32[20,18,1,128]{3,2,1,0:T(1,128)} %get-tuple-element.111), channel_id=1, source_target_pairs={{0,1},{1,2},{2,3},{3,4},{4,5},{5,6},{6,7},{7,8},{8,9},{9,10},{10,1... | collective-permute-start | bytes 552968 | tf_op jit(solution)/shard_map/ppermute | solution.py:44
  52.0 5.6 %collective-permute-start.3 = (f32[20,18,1,128]{3,2,1,0:T(1,128)}, f32[20,18,1,128]{3,2,1,0:T(1,128)}, u32[]{:S(2)}, u32[]{:S(2)}) collective-permute-start(f32[20,18,1,128]{3,2,1,0:T(1,128)} %get-tuple-element.112), channel_id=1, source_target_pairs={{1,0},{2,1},{3,2},{4,3},{5,4},{6,5},{7,6},{8,7},{9,8},{10,9},{11,1... | collective-permute-start | bytes 552968 | tf_op jit(solution)/shard_map/ppermute | solution.py:46
  55.1 2.5 slice-start.5
  58.7 1.8 copy-start.7
  58.7 1.8 copy-start.11
  58.7 1.8 copy-start.18
  58.7 1.8 copy-start.19
  58.8 1.8 copy-start.20
  58.8 1.8 copy-start.21
  65.7 49.5 %copy-start.8 = (f32[16,32,128]{2,1,0:T(8,128)}, f32[16,32,128]{2,1,0:T(8,128)S(1)}, u32[]{:S(2)}) copy-start(f32[16,32,128]{2,1,0:T(8,128)S(1)} %get-tuple-element.50) | copy-start | bytes 786436
  65.9 49.1 %copy-start.12 = (f32[16,32,128]{2,1,0:T(8,128)}, f32[16,32,128]{2,1,0:T(8,128)S(1)}, u32[]{:S(2)}) copy-start(f32[16,32,128]{2,1,0:T(8,128)S(1)} %get-tuple-element.48) | copy-start | bytes 786436
  67.5 6.0 %copy-start.25 = (s32[128,32]{1,0:T(8,128)S(1)}, s32[128,32]{1,0:T(8,128)}, u32[]{:S(2)}) copy-start(s32[128,32]{1,0:T(8,128)} %copy.26) | copy-start | bytes 49156
  67.7 6.6 %copy-start.26 = (s32[128,32]{1,0:T(8,128)S(1)}, s32[128,32]{1,0:T(8,128)}, u32[]{:S(2)}) copy-start(s32[128,32]{1,0:T(8,128)} %get-tuple-element.14) | copy-start | bytes 49156
  68.6 2.3 copy-start.3
  71.0 16.1 %collective-permute-start.4 = (f32[20,1,32,128]{3,2,1,0:T(8,128)S(1)}, f32[20,1,32,128]{3,2,1,0:T(8,128)S(1)}, u32[]{:S(2)}, u32[]{:S(2)}) collective-permute-start(f32[20,1,32,128]{3,2,1,0:T(8,128)S(1)} %get-tuple-element.126), channel_id=1, source_target_pairs={{0,16},{16,32},{32,48},{48,64},{64,80},{80,96},{96,112},{112,0},{1... | collective-permute-start | bytes 983048 | tf_op jit(solution)/shard_map/ppermute | solution.py:44
  72.7 24.2 %collective-permute-start.5 = (f32[20,1,32,128]{3,2,1,0:T(8,128)S(1)}, f32[20,1,32,128]{3,2,1,0:T(8,128)S(1)}, u32[]{:S(2)}, u32[]{:S(2)}) collective-permute-start(f32[20,1,32,128]{3,2,1,0:T(8,128)S(1)} %get-tuple-element.127), channel_id=1, source_target_pairs={{16,0},{32,16},{48,32},{64,48},{80,64},{96,80},{112,96},{0,112},{1... | collective-permute-start | bytes 983048 | tf_op jit(solution)/shard_map/ppermute | solution.py:46
  99.7 17.8 %slice-start.2 = ((s8[5242880]{0:T(1024)(128)(4,1)}), s8[1048576]{0:T(1024)(128)(4,1)S(1)}, s32[]{:S(2)}) async-start(s8[5242880]{0:T(1024)(128)(4,1)} %bitcast.604), calls=%async_computation.3 | async-start | bytes 2097152
  99.7 17.5 %collective-permute-start.6 = (f32[20,18,1,128]{3,2,1,0:T(1,128)}, f32[20,18,1,128]{3,2,1,0:T(1,128)S(1)}, u32[]{:S(2)}, u32[]{:S(2)}) collective-permute-start(f32[20,18,1,128]{3,2,1,0:T(1,128)} %get-tuple-element.107), channel_id=1, source_target_pairs={{0,1},{1,2},{2,3},{3,4},{4,5},{5,6},{6,7},{7,8},{8,9},{9,10},{10,1... | collective-permute-start | bytes 552968 | tf_op jit(solution)/shard_map/ppermute | solution.py:44
  112.2 5.3 %collective-permute-start.7 = (f32[20,18,1,128]{3,2,1,0:T(1,128)}, f32[20,18,1,128]{3,2,1,0:T(1,128)}, u32[]{:S(2)}, u32[]{:S(2)}) collective-permute-start(f32[20,18,1,128]{3,2,1,0:T(1,128)} %get-tuple-element.108), channel_id=1, source_target_pairs={{1,0},{2,1},{3,2},{4,3},{5,4},{6,5},{7,6},{8,7},{9,8},{10,9},{11,1... | collective-permute-start | bytes 552968 | tf_op jit(solution)/shard_map/ppermute | solution.py:46
  115.3 2.6 slice-start.3
  119.0 1.7 copy-start.9
  119.0 1.7 copy-start.13
  119.0 1.7 copy-start.16
  119.0 1.7 copy-start.17
  128.1 37.8 %copy-start.2 = (f32[20,16,32,128]{3,2,1,0:T(8,128)}, f32[20,16,32,128]{3,2,1,0:T(8,128)S(1)}, u32[]{:S(2)}) copy-start(f32[20,16,32,128]{3,2,1,0:T(8,128)S(1)} %bitcast_dynamic-update-slice_fusion) | copy-start | bytes 15728644
  128.2 18.1 %collective-permute-start.8 = (f32[20,1,32,128]{3,2,1,0:T(8,128)S(1)}, f32[20,1,32,128]{3,2,1,0:T(8,128)S(1)}, u32[]{:S(2)}, u32[]{:S(2)}) collective-permute-start(f32[20,1,32,128]{3,2,1,0:T(8,128)S(1)} %get-tuple-element.124), channel_id=1, source_target_pairs={{0,16},{16,32},{32,48},{48,64},{64,80},{80,96},{96,112},{112,0},{1... | collective-permute-start | bytes 983048 | tf_op jit(solution)/shard_map/ppermute | solution.py:44
  128.3 20.6 %collective-permute-start.9 = (f32[20,1,32,128]{3,2,1,0:T(8,128)S(1)}, f32[20,1,32,128]{3,2,1,0:T(8,128)S(1)}, u32[]{:S(2)}, u32[]{:S(2)}) collective-permute-start(f32[20,1,32,128]{3,2,1,0:T(8,128)S(1)} %get-tuple-element.123), channel_id=1, source_target_pairs={{16,0},{32,16},{48,32},{64,48},{80,64},{96,80},{112,96},{0,112},{1... | collective-permute-start | bytes 983048 | tf_op jit(solution)/shard_map/ppermute | solution.py:46
  149.1 16.8 %collective-permute-start.10 = (f32[20,18,1,128]{3,2,1,0:T(1,128)S(1)}, f32[20,18,1,128]{3,2,1,0:T(1,128)S(1)}, u32[]{:S(2)}, u32[]{:S(2)}) collective-permute-start(f32[20,18,1,128]{3,2,1,0:T(1,128)S(1)} %get-tuple-element.104), channel_id=1, source_target_pairs={{0,1},{1,2},{2,3},{3,4},{4,5},{5,6},{6,7},{7,8},{8,9},{9,10},{10,1... | collective-permute-start | bytes 552968 | tf_op jit(solution)/shard_map/ppermute | solution.py:44
  151.4 14.5 %collective-permute-start.11 = (f32[20,18,1,128]{3,2,1,0:T(1,128)S(1)}, f32[20,18,1,128]{3,2,1,0:T(1,128)S(1)}, u32[]{:S(2)}, u32[]{:S(2)}) collective-permute-start(f32[20,18,1,128]{3,2,1,0:T(1,128)S(1)} %get-tuple-element.103), channel_id=1, source_target_pairs={{1,0},{2,1},{3,2},{4,3},{5,4},{6,5},{7,6},{8,7},{9,8},{10,9},{11,1... | collective-permute-start | bytes 552968 | tf_op jit(solution)/shard_map/ppermute | solution.py:46
  165.9 0.7 copy-start.24
  212.9 3.6 %copy-start.22 = (f32[16,32,1]{2,1,0:T(8,128)S(1)}, f32[16,32,1]{2,1,0:T(8,128)}, u32[]{:S(2)}) copy-start(f32[16,32,1]{2,1,0:T(8,128)} %slice.981) | copy-start | bytes 6148
  212.9 5.3 %slice-start = ((s8[5242880]{0:T(1024)(128)(4,1)}), s8[4194304]{0:T(1024)(128)(4,1)S(1)}, s32[]{:S(2)}) async-start(s8[5242880]{0:T(1024)(128)(4,1)} %bitcast.602), calls=%async_computation.1 | async-start | bytes 8388608
  214.7 3.5 slice-start.1
  220.5 5.3 %copy-start.14 = (f32[16,32,128]{2,1,0:T(8,128)}, f32[16,32,128]{2,1,0:T(8,128)S(1)}, u32[]{:S(2)}) copy-start(f32[16,32,128]{2,1,0:T(8,128)S(1)} %get-tuple-element.114) | copy-start | bytes 786436
  221.3 4.6 %copy-start.30 = (pred[128,32]{1,0:T(8,128)(4,1)S(1)}, pred[128,32]{1,0:T(8,128)(4,1)}, u32[]{:S(2)}) copy-start(pred[128,32]{1,0:T(8,128)(4,1)} %get-tuple-element.13) | copy-start | bytes 12292
  222.2 3.6 %copy-start.15 = (f32[16,32,128]{2,1,0:T(8,128)}, f32[16,32,128]{2,1,0:T(8,128)S(1)}, u32[]{:S(2)}) copy-start(f32[16,32,128]{2,1,0:T(8,128)S(1)} %get-tuple-element.116) | copy-start | bytes 786436
  267.8 13.6 %copy-start.28 = (bf16[128,128]{0,1:T(8,128)(2,1)S(1)}, bf16[128,128]{0,1:T(8,128)(2,1)}, u32[]{:S(2)}) copy-start(bf16[128,128]{0,1:T(8,128)(2,1)} %copy.25) | copy-start | bytes 98308
  267.8 54.8 %copy-start.31 = (pred[128,32]{1,0:T(8,128)(4,1)S(1)}, pred[128,32]{1,0:T(8,128)(4,1)}, u32[]{:S(2)}) copy-start(pred[128,32]{1,0:T(8,128)(4,1)} %get-tuple-element.16) | copy-start | bytes 12292
  269.7 53.0 %copy-start.29 = (s32[4096,1]{0,1:T(1,128)S(1)}, s32[4096,1]{0,1:T(1,128)}, u32[]{:S(2)}) copy-start(s32[4096,1]{0,1:T(1,128)} %compare_select_fusion.2) | copy-start | bytes 49156
  351.6 0.7 copy-start.1
Sparse Core Ops, SparseCore 0:
  24.7 122.2 all-gather.1
where the time goes:
time: 360 us; the launch traced here: 359 us
  other arithmetic  93.7 us (26%)
  blocking collectives  78.3 us (22%)
  local copies, waits for them, and re-layouts  69.8 us (19%)
  waiting for transfers between devices  54.9 us (15%)
  starting transfers between devices  41.8 us (12%)
  between operations  15 us (4%)
  matrix products  5.62 us (2%)
    unnamed x75, other arithmetic  43.6 us
    psum x1, blocking collectives, per_device(): inlet_mean = lax.psum(partial_inlet, 'tile') / intake_face_position.shape[1]  39.8 us
    psum x1, blocking collectives, per_device(): exhaust = lax.psum(partial_exhaust, 'tile')  38.5 us
    ppermute x6, waiting for transfers between devices, extended(): lax.ppermute(tail, axis, [(i, (i + 1) % count) for i in range(count)])  37.3 us
    scatter-add x1, other arithmetic, per_device(): flat_heat = flat_heat.at[exhaust_index.reshape(-1)].add(change.reshape(-1))  28.9 us
    gather x2, local copies, waits for them, and re-layouts, per_device(): flat_heat[inlet_index]  23.1 us
    gather x2, local copies, waits for them, and re-layouts, per_device(): old_values = flat_heat[exhaust_index]  23.1 us
    ppermute x6, starting transfers between devices, extended(): lax.ppermute(head, axis, [((i + 1) % count, i) for i in range(count)])  21.4 us
  transfers between devices with their start and end apart: 13, of which 8 were waited for; matrix products, arithmetic and copies ran while one was open for 32% of the time, Pallas kernels for 0%

commit v1 on v0

--- a/solution.py
+++ b/solution.py
@@ -180,7 +180,7 @@
     read_rows = jnp.dot(kind_hot, read_table, precision=lax.Precision.HIGHEST)
     new_states = keep_share * state_rows + mixed + gain_rows * inlet_mean[:, None]
     partial_exhaust = jnp.sum(read_rows * new_states, axis=1)
-    exhaust = lax.psum(partial_exhaust, "tile")
+    exhaust = jnp.sum(lax.all_gather(partial_exhaust, "tile"), axis=0)
     block_exhaust = lax.dynamic_slice_in_dim(outflow_face_position, first_rack, block_racks, 0)
     exhaust_owned, exhaust_index = locate(block_exhaust)
     old_values = flat_heat[exhaust_index]

time: 360 us -> 347 us (0.964)
  blocking collectives: 78.3 us -> 64.5 us
  starting transfers between devices: 41.8 us -> 37.2 us
    psum x1 -> x0, blocking collectives: 38.5 us -> none  [per_device(): exhaust = lax.psum(partial_exhaust, 'tile')]
    all_gather x0 -> x1, blocking collectives: none -> 24.6 us  [per_device(): exhaust = jnp.sum(lax.all_gather(partial_exhaust, 'tile'), axis=0)]
    ppermute x6, waiting for transfers between devices: 37.3 us -> 48.9 us  [extended(): lax.ppermute(tail, axis, [(i, (i + 1) % count) for i in range(count)])]
    ppermute x6, waiting for transfers between devices: 17.6 us -> 6.98 us  [extended(): lax.ppermute(head, axis, [((i + 1) % count, i) for i in range(count)])]
    unnamed x81 -> x83, local copies, waits for them, and re-layouts: 9.84 us -> 10.1 us
  transfers between devices with their start and end apart: 13 -> 13, of which waited for: 8 -> 6; matrix products, arithmetic and copies ran while one was open for 32% -> 34% of each run, Pallas kernels for 0% -> 0%
where the time goes in v1:
time: 347 us; the launch traced here: 343 us
  other arithmetic  93.6 us (27%)
  local copies, waits for them, and re-layouts  70.8 us (20%)
  blocking collectives  64.5 us (19%)
  waiting for transfers between devices  55.9 us (16%)
  starting transfers between devices  37.2 us (11%)
  between operations  15 us (4%)
  matrix products  5.61 us (2%)
    ppermute x6, waiting for transfers between devices, extended(): lax.ppermute(tail, axis, [(i, (i + 1) % count) for i in range(count)])  48.9 us
    unnamed x75, other arithmetic  43.6 us
    psum x1, blocking collectives, per_device(): inlet_mean = lax.psum(partial_inlet, 'tile') / intake_face_position.shape[1]  39.9 us
    scatter-add x1, other arithmetic, per_device(): flat_heat = flat_heat.at[exhaust_index.reshape(-1)].add(change.reshape(-1))  28.9 us
    all_gather x1, blocking collectives, per_device(): exhaust = jnp.sum(lax.all_gather(partial_exhaust, 'tile'), axis=0)  24.6 us
    gather x2, local copies, waits for them, and re-layouts, per_device(): flat_heat[inlet_index]  23.1 us
    gather x2, local copies, waits for them, and re-layouts, per_device(): old_values = flat_heat[exhaust_index]  23.1 us
    ppermute x6, starting transfers between devices, extended(): lax.ppermute(tail, axis, [(i, (i + 1) % count) for i in range(count)])  18.9 us
  transfers between devices with their start and end apart: 13, of which 6 were waited for; matrix products, arithmetic and copies ran while one was open for 34% of the time, Pallas kernels for 0%

profile of v1, /device:TPU:7, one launch (start us, length us, event | category | flops | bytes accessed | tf_op | source)
XLA Modules:
  0.0 342.7 jit_solution(14094817974932600)
XLA Ops:
  7.2 3.0 reduce_sum.193
  10.3 4.1 %bitcast_dynamic-update-slice_fusion.10 = (f32[20,16,32,128]{3,2,1,0:T(8,128)S(1)}, f32[16,32,128]{2,1,0:T(8,128)}, f32[16,32,128]{2,1,0:T(8,128)S(1)}, f32[16,3...) fusion(f32[16,32,128]{2,1,0:T(8,128)S(1)} %reduce_sum.193, ...), kind=kLoop, calls=%fused_computation.703 | loop fusion | flops 4521983 | bytes 7667712
  14.4 1.2 fusion.20
  19.7 2.3 copy-done.4
  22.1 1.4 collective-permute-start
  23.4 1.1 collective-permute-start.1
  24.5 0.7 constant_dynamic-slice_fusion
  25.4 0.9 compare_select_fusion
  27.7 14.8 %collective-permute-done = f32[20,1,32,128]{3,2,1,0:T(8,128)S(1)} collective-permute-done((f32[20,1,32,128]{3,2,1,0:T(8,128)S(1)}, f32[20,1,32,128]{3,2,1,0:T(8,128)S(1)}, u32[]{:S(2)}, u32[]{:S(2)}) %collective-permute-start) | collective-permute-done | bytes 327712 | tf_op jit(solution)/shard_map/ppermute | solution.py:44
  42.5 4.2 %collective-permute-done.1 = f32[20,1,32,128]{3,2,1,0:T(8,128)S(1)} collective-permute-done((f32[20,1,32,128]{3,2,1,0:T(8,128)S(1)}, f32[20,1,32,128]{3,2,1,0:T(8,128)S(1)}, u32[]{:S(2)}, u32[]{:S(2)}) %collective-permute-start.1) | collective-permute-done | bytes 327712 | tf_op jit(solution)/shard_map/ppermute | solution.py:46
  46.7 2.8 pad_maximum_fusion.70
  49.5 2.5 collective-permute-start.2
  51.9 0.9 compare_select_fusion.1
  52.8 0.8 slice.921
  53.6 0.8 slice.919
  54.5 1.5 reshape.147
  56.0 1.4 fusion.507
  58.5 0.7 fusion.6
  59.6 1.0 fusion.505
  61.4 4.0 %bitcast_dynamic-update-slice_fusion.6 = (f32[20,16,32,128]{3,2,1,0:T(8,128)S(1)}, f32[16,32,128]{2,1,0:T(8,128)}, f32[16,32,128]{2,1,0:T(8,128)S(1)}, f32[16,32...) fusion(pred[16,32,128]{2,1,0:T(8,128)(4,1)S(1)} %get-tuple-elem, ...), kind=kLoop, calls=%fused_computation.699 | loop fusion | flops 9175039 | bytes 18653184
  69.5 2.3 copy-done.3
  71.9 1.7 collective-permute-start.4
  73.5 0.8 collective-permute-start.5
  75.0 24.5 %collective-permute-done.4 = f32[20,1,32,128]{3,2,1,0:T(8,128)S(1)} collective-permute-done((f32[20,1,32,128]{3,2,1,0:T(8,128)S(1)}, f32[20,1,32,128]{3,2,1,0:T(8,128)S(1)}, u32[]{:S(2)}, u32[]{:S(2)}) %collective-permute-start.4) | collective-permute-done | bytes 327712 | tf_op jit(solution)/shard_map/ppermute | solution.py:44
  99.5 2.7 pad_maximum_fusion.67
  102.2 10.4 %collective-permute-start.6 = (f32[20,18,1,128]{3,2,1,0:T(1,128)}, f32[20,18,1,128]{3,2,1,0:T(1,128)S(1)}, u32[]{:S(2)}, u32[]{:S(2)}) collective-permute-start(f32[20,18,1,128]{3,2,1,0:T(1,128)} %get-tuple-element.107), channel_id=1, source_target_pairs={{0,1},{1,2},{2,3},{3,4},{4,5},{5,6},{6,7},{7,8},{8,9},{9,10},{10,1... | collective-permute-start | bytes 552968 | tf_op jit(solution)/shard_map/ppermute | solution.py:44
  113.3 0.8 dynamic_slice.19
  114.1 1.5 copy.25
  115.8 1.4 fusion.503
  119.5 1.0 fusion.501
  121.2 3.4 constant_dynamic-update-slice_fusion
  128.7 6.0 %collective-permute-start.9 = (f32[20,1,32,128]{3,2,1,0:T(8,128)S(1)}, f32[20,1,32,128]{3,2,1,0:T(8,128)S(1)}, u32[]{:S(2)}, u32[]{:S(2)}) collective-permute-start(f32[20,1,32,128]{3,2,1,0:T(8,128)S(1)} %get-tuple-element.123), channel_id=1, source_target_pairs={{16,0},{32,16},{48,32},{64,48},{80,64},{96,80},{112,96},{0,112},{1... | collective-permute-start | bytes 983048 | tf_op jit(solution)/shard_map/ppermute | solution.py:46
  134.7 0.8 slice.981
  136.4 9.7 %collective-permute-done.8 = f32[20,1,32,128]{3,2,1,0:T(8,128)S(1)} collective-permute-done((f32[20,1,32,128]{3,2,1,0:T(8,128)S(1)}, f32[20,1,32,128]{3,2,1,0:T(8,128)S(1)}, u32[]{:S(2)}, u32[]{:S(2)}) %collective-permute-start.8) | collective-permute-done | bytes 327712 | tf_op jit(solution)/shard_map/ppermute | solution.py:44
  146.1 2.1 collective-permute-done.9
  148.5 2.9 collective-permute-start.10
  151.4 10.4 %collective-permute-start.11 = (f32[20,18,1,128]{3,2,1,0:T(1,128)S(1)}, f32[20,18,1,128]{3,2,1,0:T(1,128)S(1)}, u32[]{:S(2)}, u32[]{:S(2)}) collective-permute-start(f32[20,18,1,128]{3,2,1,0:T(1,128)S(1)} %get-tuple-element.103), channel_id=1, source_target_pairs={{1,0},{2,1},{3,2},{4,3},{5,4},{6,5},{7,6},{8,7},{9,8},{10,9},{11,1... | collective-permute-start | bytes 552968 | tf_op jit(solution)/shard_map/ppermute | solution.py:46
  163.9 23.0 %gather_fusion = f32[4096]{0:T(1024)S(1)} fusion(f32[65536]{0:T(1024)S(1)} %bitcast.599, s32[4096]{0:T(1024)S(1)} %broadcast_clamp_fusion.1), kind=kCustom, calls=%fused_computation | custom fusion | bytes 49152 | tf_op jit(solution)/shard_map/gather | solution.py:162
  187.0 23.0 %gather_fusion.1 = f32[4096]{0:T(1024)S(1)} fusion(f32[65536]{0:T(1024)S(1)} %bitcast.600, s32[4096]{0:T(1024)S(1)} %copy-done.24), kind=kCustom, calls=%fused_computation.1 | custom fusion | bytes 49152 | tf_op jit(solution)/shard_map/gather | solution.py:186
  210.2 1.8 maximum_dynamic-update-slice_fusion.5
  212.0 1.8 maximum_dynamic-update-slice_fusion.4
  213.8 0.8 fusion.509
  214.6 0.8 fusion.510
  217.0 0.9 fusion.497
  217.8 0.8 slice.985
  218.6 0.8 fusion.498
  219.5 0.8 slice.987
  220.3 0.8 slice.989
  221.2 0.8 slice.991
  222.0 0.8 slice.993
  223.4 39.9 %psum.7 = f32[128]{0:T(128)S(1)} all-reduce(f32[128]{0:T(128)S(1)} %select_reduce_fusion), channel_id=1, replica_groups=mesh['slab'=8,'tile'=16] {'tile'}, use_global_device_ids=true, to_apply=%region_3.4 | all-reduce | flops 128 | bytes 1024 | tf_op jit(solution)/shard_map/psum | solution.py:163
  263.3 1.9 fusion.511
  265.2 1.9 fusion.512
  267.0 1.8 fusion.513
  268.8 1.8 fusion.514
  270.6 1.8 fusion.515
  272.4 0.8 fusion.516
  273.3 0.8 fusion.517
  274.1 0.8 fusion.518
  274.9 3.7 %fusion = f32[128,128]{1,0:T(8,128)S(1)} fusion(bf16[8,128,2048]{2,1,0:T(8,128)(2,1)} %all-gather.4.cloned.1.call-done, bf16[128,2048]{1,0:T(8,128)(2,1)S(1)} %copy-done, f32[128,8]{0,1:T(8,128)S(1)} %fusion.571), kind=kOutput, calls=%fused_computation.4 | convolution fusion | flops 537116672 | bytes 4788224 | tf_op jit(solution)/shard_map/dot_general | solution.py:166
  278.8 0.9 fusion.1
  280.5 1.0 fusion.2
  281.4 24.6 %all-gather.1 = f32[16,1,128]{2,1,0:T(1,128)S(1)} all-gather(f32[1,1,128]{2,1,0:T(1,128)S(1)} %bitcast.640), channel_id=2, replica_groups=mesh['slab'=8,'tile'=16] {'tile'}, dimensions={0}, use_global_device_ids=true | all-gather | bytes 8704 | tf_op jit(solution)/shard_map/all_gather | solution.py:183
  306.3 28.9 %scatter_fusion = f32[65536]{0:T(1024)S(1)} fusion(f32[65536]{0:T(1024)S(1)} %bitcast.601, s32[4096]{0:T(1024)S(1)} %bitcast.639, f32[4096]{0:T(1024)S(1)} %reshape.165), kind=kCustom, calls=%fused_computation.2 | custom fusion | flops 4096 | bytes 65536 | tf_op jit(solution)/shard_map/scatter-add | solution.py:188
  (206 shorter events, 27.3 us)
Async XLA Ops:
  7.2 105.5 %copy-start = (bf16[128,2048]{1,0:T(8,128)(2,1)S(1)}, bf16[128,2048]{1,0:T(8,128)(2,1)}, u32[]{:S(2)}) copy-start(bf16[128,2048]{1,0:T(8,128)(2,1)} %param.19) | copy-start | bytes 1572868
  7.2 3.1 copy-start.23
  7.2 3.1 copy-start.27
  7.2 267.7 %all-gather.4.cloned.1.call-start = ((), (), s32[]{:S(2)}) async-start(), calls=%async_computation | async-start | bytes 4718592 | tf_op jit(solution)/shard_map/all_gather | solution.py:164
  10.3 5.3 %copy-start.5 = (f32[19,16,32,128]{3,2,1,0:T(8,128)S(1)}, f32[19,16,32,128]{3,2,1,0:T(8,128)}, u32[]{:S(2)}) copy-start(f32[19,16,32,128]{3,2,1,0:T(8,128)} %param.10) | copy-start | bytes 14942212
  16.6 37.0 %copy-start.6 = (f32[16,32,128]{2,1,0:T(8,128)}, f32[16,32,128]{2,1,0:T(8,128)S(1)}, u32[]{:S(2)}) copy-start(f32[16,32,128]{2,1,0:T(8,128)S(1)} %get-tuple-element.80) | copy-start | bytes 786436
  16.8 36.0 %copy-start.8 = (f32[16,32,128]{2,1,0:T(8,128)}, f32[16,32,128]{2,1,0:T(8,128)S(1)}, u32[]{:S(2)}) copy-start(f32[16,32,128]{2,1,0:T(8,128)S(1)} %get-tuple-element.78) | copy-start | bytes 786436
  19.7 2.3 copy-start.4
  22.1 20.4 %collective-permute-start = (f32[20,1,32,128]{3,2,1,0:T(8,128)S(1)}, f32[20,1,32,128]{3,2,1,0:T(8,128)S(1)}, u32[]{:S(2)}, u32[]{:S(2)}) collective-permute-start(f32[20,1,32,128]{3,2,1,0:T(8,128)S(1)} %get-tuple-element.129), channel_id=1, source_target_pairs={{0,16},{16,32},{32,48},{48,64},{64,80},{80,96},{96,112},{112,0},{1... | collective-permute-start | bytes 983048 | tf_op jit(solution)/shard_map/ppermute | solution.py:44
  23.4 23.2 %collective-permute-start.1 = (f32[20,1,32,128]{3,2,1,0:T(8,128)S(1)}, f32[20,1,32,128]{3,2,1,0:T(8,128)S(1)}, u32[]{:S(2)}, u32[]{:S(2)}) collective-permute-start(f32[20,1,32,128]{3,2,1,0:T(8,128)S(1)} %get-tuple-element.130), channel_id=1, source_target_pairs={{16,0},{32,16},{48,32},{64,48},{80,64},{96,80},{112,96},{0,112},{1... | collective-permute-start | bytes 983048 | tf_op jit(solution)/shard_map/ppermute | solution.py:46
  27.7 24.2 %copy-start.25 = (s32[128,32]{1,0:T(8,128)S(1)}, s32[128,32]{1,0:T(8,128)}, u32[]{:S(2)}) copy-start(s32[128,32]{1,0:T(8,128)} %copy.26) | copy-start | bytes 49156
  49.5 8.3 %slice-start.4 = ((s8[5242880]{0:T(1024)(128)(4,1)}), s8[1048576]{0:T(1024)(128)(4,1)S(1)}, s32[]{:S(2)}) async-start(s8[5242880]{0:T(1024)(128)(4,1)} %bitcast.607), calls=%async_computation.5 | async-start | bytes 2097152
  49.5 8.3 %collective-permute-start.2 = (f32[20,18,1,128]{3,2,1,0:T(1,128)}, f32[20,18,1,128]{3,2,1,0:T(1,128)S(1)}, u32[]{:S(2)}, u32[]{:S(2)}) collective-permute-start(f32[20,18,1,128]{3,2,1,0:T(1,128)} %get-tuple-element.111), channel_id=1, source_target_pairs={{0,1},{1,2},{2,3},{3,4},{4,5},{5,6},{6,7},{7,8},{8,9},{9,10},{10,1... | collective-permute-start | bytes 552968 | tf_op jit(solution)/shard_map/ppermute | solution.py:44
  51.9 5.9 %collective-permute-start.3 = (f32[20,18,1,128]{3,2,1,0:T(1,128)}, f32[20,18,1,128]{3,2,1,0:T(1,128)}, u32[]{:S(2)}, u32[]{:S(2)}) collective-permute-start(f32[20,18,1,128]{3,2,1,0:T(1,128)} %get-tuple-element.112), channel_id=1, source_target_pairs={{1,0},{2,1},{3,2},{4,3},{5,4},{6,5},{7,6},{8,7},{9,8},{10,9},{11,1... | collective-permute-start | bytes 552968 | tf_op jit(solution)/shard_map/ppermute | solution.py:46
  56.0 2.5 slice-start.5
  59.6 1.8 copy-start.7
  59.6 1.8 copy-start.9
  59.6 1.8 copy-start.18
  59.6 1.8 copy-start.19
  59.6 1.8 copy-start.20
  59.6 1.8 copy-start.21
  66.5 49.1 %copy-start.10 = (f32[16,32,128]{2,1,0:T(8,128)}, f32[16,32,128]{2,1,0:T(8,128)S(1)}, u32[]{:S(2)}) copy-start(f32[16,32,128]{2,1,0:T(8,128)S(1)} %get-tuple-element.50) | copy-start | bytes 786436
  66.8 48.8 %copy-start.12 = (f32[16,32,128]{2,1,0:T(8,128)}, f32[16,32,128]{2,1,0:T(8,128)S(1)}, u32[]{:S(2)}) copy-start(f32[16,32,128]{2,1,0:T(8,128)S(1)} %get-tuple-element.48) | copy-start | bytes 786436
  68.3 6.0 %copy-start.31 = (s32[4096]{0:T(1024)S(1)}, s32[4096]{0:T(1024)}, u32[]{:S(2)}) copy-start(s32[4096]{0:T(1024)} %reshape.147) | copy-start | bytes 49156
  68.3 6.0 %copy-start.26 = (s32[128,32]{1,0:T(8,128)S(1)}, s32[128,32]{1,0:T(8,128)}, u32[]{:S(2)}) copy-start(s32[128,32]{1,0:T(8,128)} %get-tuple-element.14) | copy-start | bytes 49156
  69.5 2.3 copy-start.3
  71.9 27.6 %collective-permute-start.4 = (f32[20,1,32,128]{3,2,1,0:T(8,128)S(1)}, f32[20,1,32,128]{3,2,1,0:T(8,128)S(1)}, u32[]{:S(2)}, u32[]{:S(2)}) collective-permute-start(f32[20,1,32,128]{3,2,1,0:T(8,128)S(1)} %get-tuple-element.126), channel_id=1, source_target_pairs={{0,16},{16,32},{32,48},{48,64},{64,80},{80,96},{96,112},{112,0},{1... | collective-permute-start | bytes 983048 | tf_op jit(solution)/shard_map/ppermute | solution.py:44
  73.5 26.0 %collective-permute-start.5 = (f32[20,1,32,128]{3,2,1,0:T(8,128)S(1)}, f32[20,1,32,128]{3,2,1,0:T(8,128)S(1)}, u32[]{:S(2)}, u32[]{:S(2)}) collective-permute-start(f32[20,1,32,128]{3,2,1,0:T(8,128)S(1)} %get-tuple-element.127), channel_id=1, source_target_pairs={{16,0},{32,16},{48,32},{64,48},{80,64},{96,80},{112,96},{0,112},{1... | collective-permute-start | bytes 983048 | tf_op jit(solution)/shard_map/ppermute | solution.py:46
  102.2 16.0 %slice-start.2 = ((s8[5242880]{0:T(1024)(128)(4,1)}), s8[1048576]{0:T(1024)(128)(4,1)S(1)}, s32[]{:S(2)}) async-start(s8[5242880]{0:T(1024)(128)(4,1)} %bitcast.605), calls=%async_computation.3 | async-start | bytes 2097152
  102.2 15.4 %collective-permute-start.6 = (f32[20,18,1,128]{3,2,1,0:T(1,128)}, f32[20,18,1,128]{3,2,1,0:T(1,128)S(1)}, u32[]{:S(2)}, u32[]{:S(2)}) collective-permute-start(f32[20,18,1,128]{3,2,1,0:T(1,128)} %get-tuple-element.107), channel_id=1, source_target_pairs={{0,1},{1,2},{2,3},{3,4},{4,5},{5,6},{6,7},{7,8},{8,9},{9,10},{10,1... | collective-permute-start | bytes 552968 | tf_op jit(solution)/shard_map/ppermute | solution.py:44
  112.7 5.6 %collective-permute-start.7 = (f32[20,18,1,128]{3,2,1,0:T(1,128)}, f32[20,18,1,128]{3,2,1,0:T(1,128)}, u32[]{:S(2)}, u32[]{:S(2)}) collective-permute-start(f32[20,18,1,128]{3,2,1,0:T(1,128)} %get-tuple-element.108), channel_id=1, source_target_pairs={{1,0},{2,1},{3,2},{4,3},{5,4},{6,5},{7,6},{8,7},{9,8},{10,9},{11,1... | collective-permute-start | bytes 552968 | tf_op jit(solution)/shard_map/ppermute | solution.py:46
  115.8 2.6 slice-start.3
  119.4 1.7 copy-start.11
  119.4 1.7 copy-start.13
  119.4 1.7 copy-start.16
  119.4 1.7 copy-start.17
  128.6 34.7 %copy-start.2 = (f32[20,16,32,128]{3,2,1,0:T(8,128)}, f32[20,16,32,128]{3,2,1,0:T(8,128)S(1)}, u32[]{:S(2)}) copy-start(f32[20,16,32,128]{3,2,1,0:T(8,128)S(1)} %bitcast_dynamic-update-slice_fusion) | copy-start | bytes 15728644
  128.6 17.5 %collective-permute-start.8 = (f32[20,1,32,128]{3,2,1,0:T(8,128)S(1)}, f32[20,1,32,128]{3,2,1,0:T(8,128)S(1)}, u32[]{:S(2)}, u32[]{:S(2)}) collective-permute-start(f32[20,1,32,128]{3,2,1,0:T(8,128)S(1)} %get-tuple-element.124), channel_id=1, source_target_pairs={{0,16},{16,32},{32,48},{48,64},{64,80},{80,96},{96,112},{112,0},{1... | collective-permute-start | bytes 983048 | tf_op jit(solution)/shard_map/ppermute | solution.py:44
  128.7 19.5 %collective-permute-start.9 = (f32[20,1,32,128]{3,2,1,0:T(8,128)S(1)}, f32[20,1,32,128]{3,2,1,0:T(8,128)S(1)}, u32[]{:S(2)}, u32[]{:S(2)}) collective-permute-start(f32[20,1,32,128]{3,2,1,0:T(8,128)S(1)} %get-tuple-element.123), channel_id=1, source_target_pairs={{16,0},{32,16},{48,32},{64,48},{80,64},{96,80},{112,96},{0,112},{1... | collective-permute-start | bytes 983048 | tf_op jit(solution)/shard_map/ppermute | solution.py:46
  148.5 14.7 %collective-permute-start.10 = (f32[20,18,1,128]{3,2,1,0:T(1,128)S(1)}, f32[20,18,1,128]{3,2,1,0:T(1,128)S(1)}, u32[]{:S(2)}, u32[]{:S(2)}) collective-permute-start(f32[20,18,1,128]{3,2,1,0:T(1,128)S(1)} %get-tuple-element.104), channel_id=1, source_target_pairs={{0,1},{1,2},{2,3},{3,4},{4,5},{5,6},{6,7},{7,8},{8,9},{9,10},{10,1... | collective-permute-start | bytes 552968 | tf_op jit(solution)/shard_map/ppermute | solution.py:44
  151.4 11.9 %collective-permute-start.11 = (f32[20,18,1,128]{3,2,1,0:T(1,128)S(1)}, f32[20,18,1,128]{3,2,1,0:T(1,128)S(1)}, u32[]{:S(2)}, u32[]{:S(2)}) collective-permute-start(f32[20,18,1,128]{3,2,1,0:T(1,128)S(1)} %get-tuple-element.103), channel_id=1, source_target_pairs={{1,0},{2,1},{3,2},{4,3},{5,4},{6,5},{7,6},{8,7},{9,8},{10,9},{11,1... | collective-permute-start | bytes 552968 | tf_op jit(solution)/shard_map/ppermute | solution.py:46
  163.9 23.1 %copy-start.24 = (s32[4096]{0:T(1024)S(1)}, s32[4096]{0:T(1024)}, u32[]{:S(2)}) copy-start(s32[4096]{0:T(1024)} %broadcast_clamp_fusion) | copy-start | bytes 49156
  210.2 3.6 %copy-start.22 = (f32[16,32,1]{2,1,0:T(8,128)S(1)}, f32[16,32,1]{2,1,0:T(8,128)}, u32[]{:S(2)}) copy-start(f32[16,32,1]{2,1,0:T(8,128)} %slice.981) | copy-start | bytes 6148
  210.2 5.3 %slice-start = ((s8[5242880]{0:T(1024)(128)(4,1)}), s8[4194304]{0:T(1024)(128)(4,1)S(1)}, s32[]{:S(2)}) async-start(s8[5242880]{0:T(1024)(128)(4,1)} %bitcast.603), calls=%async_computation.1 | async-start | bytes 8388608
  212.0 3.5 %slice-start.1 = ((s8[5242880]{0:T(1024)(128)(4,1)}), s8[1048576]{0:T(1024)(128)(4,1)S(1)}, s32[]{:S(2)}) async-start(s8[5242880]{0:T(1024)(128)(4,1)} %bitcast.603), calls=%async_computation.2 | async-start | bytes 2097152
  217.8 5.3 %copy-start.14 = (f32[16,32,128]{2,1,0:T(8,128)}, f32[16,32,128]{2,1,0:T(8,128)S(1)}, u32[]{:S(2)}) copy-start(f32[16,32,128]{2,1,0:T(8,128)S(1)} %get-tuple-element.114) | copy-start | bytes 786436
  218.6 4.6 %copy-start.30 = (pred[128,32]{1,0:T(8,128)(4,1)S(1)}, pred[128,32]{1,0:T(8,128)(4,1)}, u32[]{:S(2)}) copy-start(pred[128,32]{1,0:T(8,128)(4,1)} %get-tuple-element.13) | copy-start | bytes 12292
  219.5 3.6 %copy-start.15 = (f32[16,32,128]{2,1,0:T(8,128)}, f32[16,32,128]{2,1,0:T(8,128)S(1)}, u32[]{:S(2)}) copy-start(f32[16,32,128]{2,1,0:T(8,128)S(1)} %get-tuple-element.116) | copy-start | bytes 786436
  265.2 13.6 %copy-start.28 = (bf16[128,128]{0,1:T(8,128)(2,1)S(1)}, bf16[128,128]{0,1:T(8,128)(2,1)}, u32[]{:S(2)}) copy-start(bf16[128,128]{0,1:T(8,128)(2,1)} %copy.25) | copy-start | bytes 98308
  265.2 40.9 %copy-start.32 = (pred[128,32]{1,0:T(8,128)(4,1)S(1)}, pred[128,32]{1,0:T(8,128)(4,1)}, u32[]{:S(2)}) copy-start(pred[128,32]{1,0:T(8,128)(4,1)} %get-tuple-element.16) | copy-start | bytes 12292
  267.0 39.2 %copy-start.29 = (s32[4096,1]{0,1:T(1,128)S(1)}, s32[4096,1]{0,1:T(1,128)}, u32[]{:S(2)}) copy-start(s32[4096,1]{0,1:T(1,128)} %compare_select_fusion.2) | copy-start | bytes 49156
  335.2 0.7 copy-start.1
Sparse Core Ops, SparseCore 0:
  24.7 119.5 all-gather.3
